TPU v7x, 512 devices: a whole 4x8x8 slice. The times are simulated.
512 devices in a mesh: gx: 16 (over y_hi, x, core), gy: 4 (over y_lo), gz: 8 (over z).
Axes of the slice: x: 4, y: 8 (y_hi: 2, y_lo: 4; y = y_hi * 4 + y_lo), z: 8, core: 2. Of those that a mesh axis runs over, the one named last changes fastest.
Arguments:
- velocity: float32 [3, 32, 4, 32, 512], P(None, 'gx', 'gy', 'gz'), may hold values from -4 to 4
- reaction: float32 [32, 4, 32, 512], P('gx', 'gy', 'gz'), may hold values from 10 to 100
Outputs:
- velocity_out: float32 [3, 32, 4, 32, 512], P(None, 'gx', 'gy', 'gz')
- pressure: float32 [32, 4, 32, 512], P('gx', 'gy', 'gz')
- residual: float32 [32, 4, 32, 512], P('gx', 'gy', 'gz')
All inputs are finite; a program needn't handle non-finite values.
Results may differ from a plain program's by a relative error of at most 0.007.
Values sent between devices are 32-bit elements; how exact they have to be, the bound alone decides.
A program may use at most 64 MiB of HBM per device.

v0:
```python
import jax
import jax.numpy as jnp
import numpy as np
from jax import lax
from jax.sharding import PartitionSpec as P

SUBSTEPS = 2
ITERS = 4
step_size = 0.02


def extended(block, sides, width, periodic):
    for axis, dim in sides:
        count = lax.axis_size(axis)
        forward = [(i, i + 1) for i in range(count - 1)]
        if periodic:
            forward.append((count - 1, 0))
        backward = [(target, source) for source, target in forward]
        low = lax.ppermute(
            lax.slice_in_dim(block, block.shape[dim] - width, None, axis=dim), axis, forward
        )
        high = lax.ppermute(lax.slice_in_dim(block, 0, width, axis=dim), axis, backward)
        block = jnp.concatenate([low, block, high], axis=dim)
    return block


def legendre_seven(points):
    earlier = points * 0.0 + 1.0
    current = points
    for degree in range(1, 7):
        earlier, current = (
            current,
            ((2 * degree + 1) * points * current - degree * earlier) / (degree + 1),
        )
    return current


def tables():
    half = np.array([0.20929921790247888, 0.5917001814331423, 0.8717401485096066, 1.0])
    points = np.concatenate([-half[::-1], half])
    legendre = legendre_seven(points)
    weights = 2.0 / (56.0 * legendre**2)
    spacing = points[:, None] - points[None, :] + np.eye(8)
    derivative = legendre[:, None] / legendre[None, :] / spacing * (1.0 - np.eye(8))
    derivative[0, 0] = -14.0
    derivative[7, 7] = 14.0
    return (jnp.asarray(weights, jnp.float32), jnp.asarray(derivative, jnp.float32))


def derive(values, derivative, along_dim, transposed):
    layout = values.shape
    matrix = derivative.T if transposed else derivative
    blocks = values.reshape(-1, 8, 8, 8)
    patterns = ("aq,nqbc->nabc", "bq,naqc->nabc", "cq,nabq->nabc")
    result = jnp.einsum(patterns[along_dim], matrix, blocks, precision=lax.Precision.HIGHEST)
    return result.reshape(layout)


def place_face(values, target_axis, position, update):
    selector = tuple(
        (position if place == target_axis else slice(None) for place in range(values.ndim))
    )
    return values.at[selector].set(update)


def faces_along_x(sequence):
    return extended(sequence, (("gx", 0),), 1, True)


def faces_along_y(sequence):
    return extended(sequence, (("gy", 0),), 1, False)


def faces_along_z(sequence):
    return extended(sequence, (("gz", 0),), 1, False)


def join_faces(values, along_dim, exchanger):
    lower_face = jnp.moveaxis(jnp.take(values, 0, axis=4 + along_dim), 1 + along_dim, 0)
    upper_face = jnp.moveaxis(jnp.take(values, 7, axis=4 + along_dim), 1 + along_dim, 0)
    elements = lower_face.shape[0]
    face_shape = lower_face.shape
    sequence = jnp.stack([lower_face, upper_face], axis=1).reshape(2 * elements, -1)
    padded = exchanger(sequence)
    paired = padded.reshape(elements + 1, 2, -1)
    totals = paired[:, 0] + paired[:, 1]
    new_lower = jnp.moveaxis(totals[:-1].reshape(face_shape), 0, 1 + along_dim)
    new_upper = jnp.moveaxis(totals[1:].reshape(face_shape), 0, 1 + along_dim)
    values = place_face(values, 4 + along_dim, 0, new_lower)
    return place_face(values, 4 + along_dim, 7, new_upper)


def assemble(values):
    exchangers = (faces_along_x, faces_along_y, faces_along_z)
    dim_order = (0, 1, 2)
    for along_dim in dim_order:
        values = join_faces(values, along_dim, exchangers[along_dim])
    return values


def dim_factors(local_count, offset, total_count, bounded_by_walls):
    element_ids = offset + jnp.arange(local_count)
    node_ids = jnp.arange(8)
    at_end = (node_ids[None, :] == 0) | (node_ids[None, :] == 7)
    low_wall = (element_ids[:, None] == 0) & (node_ids[None, :] == 0)
    high_wall = (element_ids[:, None] == total_count - 1) & (node_ids[None, :] == 7)
    on_wall = (low_wall | high_wall) & bounded_by_walls
    shared = at_end & jnp.logical_not(on_wall)
    return (jnp.where(shared, 2.0, 1.0).astype(jnp.float32), on_wall.astype(jnp.float32))


def body(velocity, reaction):
    weights, derivative = tables()
    count_x, count_y, count_z = (reaction.shape[0], reaction.shape[1], reaction.shape[2])
    speed = velocity.reshape(3, count_x, count_y, count_z, 8, 8, 8)
    react = reaction.reshape(1, count_x, count_y, count_z, 8, 8, 8)
    mass_matrix = weights[:, None, None] * weights[None, :, None] * weights[None, None, :]
    factor_x, wall_x = dim_factors(
        count_x, lax.axis_index("gx") * count_x, lax.axis_size("gx") * count_x, False
    )
    factor_y, wall_y = dim_factors(
        count_y, lax.axis_index("gy") * count_y, lax.axis_size("gy") * count_y, True
    )
    factor_z, wall_z = dim_factors(
        count_z, lax.axis_index("gz") * count_z, lax.axis_size("gz") * count_z, True
    )
    multiplicity = (
        factor_x[None, :, None, None, :, None, None]
        * factor_y[None, None, :, None, None, :, None]
        * factor_z[None, None, None, :, None, None, :]
    )
    interior = (1.0 - wall_y[None, None, :, None, None, :, None]) * (
        1.0 - wall_z[None, None, None, :, None, None, :]
    )
    stiff_sum = jnp.sum(weights[:, None] * derivative * derivative, axis=0)
    diag_local = (
        stiff_sum[:, None, None] * weights[None, :, None] * weights[None, None, :]
        + weights[:, None, None] * stiff_sum[None, :, None] * weights[None, None, :]
        + weights[:, None, None] * weights[None, :, None] * stiff_sum[None, None, :]
    )
    diag_terms = diag_local + react * mass_matrix
    speed = assemble(speed) / multiplicity
    diagonal = None
    for substep in range(SUBSTEPS):
        gradient_fields = [derive(speed, derivative, along_dim, False) for along_dim in range(3)]
        transport = (
            speed[0:1] * gradient_fields[0]
            + speed[1:2] * gradient_fields[1]
            + speed[2:3] * gradient_fields[2]
        )
        tendency = assemble(mass_matrix * transport) / (mass_matrix * multiplicity)
        speed = interior * (speed - step_size * tendency)
    spread = (
        derive(speed[0:1], derivative, 0, False)
        + derive(speed[1:2], derivative, 1, False)
        + derive(speed[2:3], derivative, 2, False)
    )
    source = -assemble(mass_matrix * spread)
    diagonal = assemble(diag_terms)

    def local_inner(first, second):
        return jnp.sum(first * second / multiplicity)

    def norm_weighted_mass(residual_vec, precond_vec):
        return lax.psum(local_inner(residual_vec, precond_vec), ("gx", "gy", "gz"))

    pressure = jnp.zeros_like(source)
    residual = source
    precond = residual / diagonal
    search = precond
    progress = norm_weighted_mass(residual, precond)
    for sweep_index in range(ITERS):
        local_sum = react * mass_matrix * search
        for apply_along_dim in range(3):
            local_sum = local_sum + derive(
                mass_matrix * derive(search, derivative, apply_along_dim, False),
                derivative,
                apply_along_dim,
                True,
            )
        applied = assemble(local_sum)
        step_length = progress / lax.psum(local_inner(search, applied), ("gx", "gy", "gz"))
        pressure = pressure + step_length * search
        residual = residual - step_length * applied
        precond = residual / diagonal
        progress_next = norm_weighted_mass(residual, precond)
        search = precond + progress_next / progress * search
        progress = progress_next
    return (
        speed.reshape(3, count_x, count_y, count_z, 512),
        pressure.reshape(count_x, count_y, count_z, 512),
        residual.reshape(count_x, count_y, count_z, 512),
    )


def solution(mesh):
    in_specs = (P(None, "gx", "gy", "gz", None), P("gx", "gy", "gz", None))
    out_specs = (
        P(None, "gx", "gy", "gz", None),
        P("gx", "gy", "gz", None),
        P("gx", "gy", "gz", None),
    )
    return jax.shard_map(body, mesh=mesh, in_specs=in_specs, out_specs=out_specs, check_vma=False)
```

profile of v0, /device:TPU:1, one launch (start us, length us, event | category | flops | bytes accessed | tf_op | source)
XLA Modules:
  0.0 1127.1 jit_solution(3727668878768256225)
XLA Ops:
  2.1 4.5 collective-permute-start
  6.6 6.2 collective-permute-start.1
  15.8 9.7 collective-permute-start.25
  30.0 4.0 collective-permute-start.2
  35.4 3.0 collective-permute-done.3
  46.6 3.0 collective-permute-done.5
  51.0 2.6 scatter.186
  54.8 15.4 %scatter.189 = f32[3,2,1,4,8,8,8]{6,5,4,3,1,0,2:T(8,128)S(1)} dynamic-update-slice(f32[3,2,1,4,8,8,8]{6,5,4,3,1,0,2:T(8,128)S(1)} %scatter.186, f32[3,2,1,4,8,8,1]{6,5,4,3,1,0,2:T(8,128)S(1)} %copy.186, s32[]{:T(128)} %constant.1319.clone.1, s32[]{:T(128)} %constant.1319.clone.1, s32[]{:T(128)} %constant.1319.clone.1, s32[]{:T(128)} %constant.1319.clone.1, s32[]{:T(128)} %constant.1319.clone.1, ...) | dynamic-update-slice | bytes 12292 | tf_op jit(solution)/shard_map/scatter | solution.py:63
  76.7 2.4 fusion.2
  79.4 2.2 collective-permute-start.6
  81.6 12.9 %collective-permute-start.7 = (f32[1,768]{1,0:T(1,128)S(1)}, f32[1,768]{1,0:T(1,128)S(1)}, u32[]{:S(2)}, u32[]{:S(2)}) collective-permute-start(f32[1,768]{1,0:T(1,128)S(1)} %get-tuple-element.938), channel_id=1, source_target_pairs={{32,0},{64,32},{96,64},{128,96},{160,128},{192,160},{224,192},{256... | collective-permute-start | bytes 9224 | tf_op jit(solution)/shard_map/ppermute | solution.py:22
  95.9 3.2 collective-permute-start.8
  100.8 2.8 collective-permute-done.9
  109.1 4.0 collective-permute-start.10
  114.5 4.7 collective-permute-done.11
  120.1 2.1 copy.201
  122.1 2.6 scatter.196
  127.5 15.4 %scatter.199 = f32[3,2,1,4,8,8,8]{6,5,4,3,1,0,2:T(8,128)S(1)} dynamic-update-slice(f32[3,2,1,4,8,8,8]{6,5,4,3,1,0,2:T(8,128)S(1)} %scatter.196, f32[3,2,1,4,8,8,1]{6,5,4,3,1,0,2:T(8,128)S(1)} %copy.203, s32[]{:T(128)} %constant.1319.clone.1, s32[]{:T(128)} %constant.1319.clone.1, s32[]{:T(128)} %constant.1319.clone.1, s32[]{:T(128)} %constant.1319.clone.1, s32[]{:T(128)} %constant.1319.clone.1, ...) | dynamic-update-slice | bytes 12292 | tf_op jit(solution)/shard_map/scatter | solution.py:63
  148.1 2.2 fusion.5
  152.4 12.7 %collective-permute-start.13 = (f32[1,768]{1,0:T(1,128)S(1)}, f32[1,768]{1,0:T(1,128)S(1)}, u32[]{:S(2)}, u32[]{:S(2)}) collective-permute-start(f32[1,768]{1,0:T(1,128)S(1)} %get-tuple-element.930), channel_id=1, source_target_pairs={{32,0},{64,32},{96,64},{128,96},{160,128},{192,160},{224,192},{256... | collective-permute-start | bytes 9224 | tf_op jit(solution)/shard_map/ppermute | solution.py:22
  165.2 4.8 collective-permute-start.28
  171.9 3.2 collective-permute-start.14
  177.0 2.6 collective-permute-done.15
  185.1 4.3 collective-permute-start.16
  190.7 3.0 collective-permute-done.17
  195.1 2.6 scatter.206
  199.0 15.4 %scatter.209 = f32[3,2,1,4,8,8,8]{6,5,4,3,1,0,2:T(8,128)S(1)} dynamic-update-slice(f32[3,2,1,4,8,8,8]{6,5,4,3,1,0,2:T(8,128)S(1)} %scatter.206, f32[3,2,1,4,8,8,1]{6,5,4,3,1,0,2:T(8,128)S(1)} %copy.220, s32[]{:T(128)} %constant.1319.clone.1, s32[]{:T(128)} %constant.1319.clone.1, s32[]{:T(128)} %constant.1319.clone.1, s32[]{:T(128)} %constant.1319.clone.1, s32[]{:T(128)} %constant.1319.clone.1, ...) | dynamic-update-slice | bytes 12292 | tf_op jit(solution)/shard_map/scatter | solution.py:63
  219.2 12.8 %collective-permute-start.19 = (f32[1,256]{1,0:T(1,128)S(1)}, f32[1,256]{1,0:T(1,128)S(1)}, u32[]{:S(2)}, u32[]{:S(2)}) collective-permute-start(f32[1,256]{1,0:T(1,128)S(1)} %get-tuple-element.992), channel_id=1, source_target_pairs={{32,0},{64,32},{96,64},{128,96},{160,128},{192,160},{224,192},{256... | collective-permute-start | bytes 3080 | tf_op jit(solution)/shard_map/ppermute | solution.py:22
  236.2 3.0 collective-permute-done.21
  240.3 3.6 collective-permute-start.22
  246.7 4.6 scatter.229
  252.8 4.8 scatter.219
  263.0 11.8 %collective-permute-start.31 = (f32[1,256]{1,0:T(1,128)S(1)}, f32[1,256]{1,0:T(1,128)S(1)}, u32[]{:S(2)}, u32[]{:S(2)}) collective-permute-start(f32[1,256]{1,0:T(1,128)S(1)} %get-tuple-element.986), channel_id=1, source_target_pairs={{32,0},{64,32},{96,64},{128,96},{160,128},{192,160},{224,192},{256... | collective-permute-start | bytes 3080 | tf_op jit(solution)/shard_map/ppermute | solution.py:22
  279.1 3.0 collective-permute-done.33
  283.2 4.3 collective-permute-start.34
  288.8 3.4 collective-permute-done.35
  293.7 4.6 scatter.239
  299.1 107.2 %all-reduce = (f32[]{:T(128)}, f32[]{:T(128)}) all-reduce(f32[]{:T(128)} %get-tuple-element.811, f32[]{:T(128)} %get-tuple-element.810), channel_id=1, replica_groups=mesh['gx'=16,'gy'=4,'gz'=8] {'gx','gy','gz'}, use_global_device_ids=true, to_apply=%region_2.15 | all-reduce | flops 2 | bytes 16 | tf_op jit(solution)/shard_map/psum | solution.py:165
  408.4 94.4 %psum.58 = f32[]{:T(128)} all-reduce(f32[]{:T(128)} %get-tuple-element.862), channel_id=1, replica_groups=mesh['gx'=16,'gy'=4,'gz'=8] {'gx','gy','gz'}, use_global_device_ids=true, to_apply=%region_6.19 | all-reduce | flops 1 | bytes 8 | tf_op jit(solution)/shard_map/psum | solution.py:165
  507.7 4.2 collective-permute-start.36
  513.9 3.2 collective-permute-done.37
  517.5 3.9 collective-permute-start.38
  522.8 3.0 collective-permute-done.39
  530.3 3.7 collective-permute-done.41
  535.5 4.6 scatter.249
  540.9 104.3 %psum.59 = f32[]{:T(128)} all-reduce(f32[]{:T(128)} %fusion.31), channel_id=1, replica_groups=mesh['gx'=16,'gy'=4,'gz'=8] {'gx','gy','gz'}, use_global_device_ids=true, to_apply=%region_8.21 | all-reduce | flops 1 | bytes 8 | tf_op jit(solution)/shard_map/psum | solution.py:182
  647.9 94.4 %psum.60 = f32[]{:T(128)} all-reduce(f32[]{:T(128)} %get-tuple-element.859), channel_id=1, replica_groups=mesh['gx'=16,'gy'=4,'gz'=8] {'gx','gy','gz'}, use_global_device_ids=true, to_apply=%region_10.23 | all-reduce | flops 1 | bytes 8 | tf_op jit(solution)/shard_map/psum | solution.py:165
  747.1 4.2 collective-permute-start.42
  753.3 3.2 collective-permute-done.43
  757.0 2.7 collective-permute-start.44
  761.1 3.0 collective-permute-done.45
  765.2 2.2 collective-permute-start.46
  768.7 3.9 collective-permute-done.47
  774.1 4.6 scatter.259
  779.5 103.8 %psum.61 = f32[]{:T(128)} all-reduce(f32[]{:T(128)} %fusion.33), channel_id=1, replica_groups=mesh['gx'=16,'gy'=4,'gz'=8] {'gx','gy','gz'}, use_global_device_ids=true, to_apply=%region_12.25 | all-reduce | flops 1 | bytes 8 | tf_op jit(solution)/shard_map/psum | solution.py:182
  886.0 94.7 %psum.62 = f32[]{:T(128)} all-reduce(f32[]{:T(128)} %get-tuple-element.856), channel_id=1, replica_groups=mesh['gx'=16,'gy'=4,'gz'=8] {'gx','gy','gz'}, use_global_device_ids=true, to_apply=%region_14.27 | all-reduce | flops 1 | bytes 8 | tf_op jit(solution)/shard_map/psum | solution.py:165
  985.5 4.2 collective-permute-start.48
  991.7 3.2 collective-permute-done.49
  995.3 2.8 collective-permute-start.50
  999.5 3.0 collective-permute-done.51
  1003.6 2.2 collective-permute-start.52
  1007.1 3.9 collective-permute-done.53
  1012.5 4.6 scatter.269
  1018.9 103.9 %psum.63 = f32[]{:T(128)} all-reduce(f32[]{:T(128)} %fusion.35), channel_id=1, replica_groups=mesh['gx'=16,'gy'=4,'gz'=8] {'gx','gy','gz'}, use_global_device_ids=true, to_apply=%region_16.29 | all-reduce | flops 1 | bytes 8 | tf_op jit(solution)/shard_map/psum | solution.py:182
  (531 shorter events, 132.6 us)
Async XLA Ops:
  1.9 10.9 copy-start.5
  2.1 27.2 %collective-permute-start = (f32[1,768]{1,0:T(1,128)S(1)}, f32[1,768]{1,0:T(1,128)S(1)}, u32[]{:S(2)}, u32[]{:S(2)}) collective-permute-start(f32[1,768]{1,0:T(1,128)S(1)} %get-tuple-element.945), channel_id=1, source_target_pairs={{0,32},{32,64},{64,96},{96,128},{128,160},{160,192},{192,224},{224... | collective-permute-start | bytes 9224 | tf_op jit(solution)/shard_map/ppermute | solution.py:19
  6.6 22.7 %collective-permute-start.1 = (f32[1,768]{1,0:T(1,128)S(1)}, f32[1,768]{1,0:T(1,128)S(1)}, u32[]{:S(2)}, u32[]{:S(2)}) collective-permute-start(f32[1,768]{1,0:T(1,128)S(1)} %get-tuple-element.946), channel_id=1, source_target_pairs={{32,0},{64,32},{96,64},{128,96},{160,128},{192,160},{224,192},{256... | collective-permute-start | bytes 9224 | tf_op jit(solution)/shard_map/ppermute | solution.py:22
  12.8 0.7 copy-start.6
  12.9 0.7 copy-start.7
  13.9 12.1 %collective-permute-start.24 = (f32[1,256]{1,0:T(1,128)S(1)}, f32[1,256]{1,0:T(1,128)S(1)}, u32[]{:S(2)}, u32[]{:S(2)}) collective-permute-start(f32[1,256]{1,0:T(1,128)S(1)} %get-tuple-element.997), channel_id=1, source_target_pairs={{0,32},{32,64},{64,96},{96,128},{128,160},{160,192},{192,224},{224... | collective-permute-start | bytes 3080 | tf_op jit(solution)/shard_map/ppermute | solution.py:19
  15.8 10.5 collective-permute-start.25
  26.7 8.7 collective-permute-start.26
  28.1 7.3 collective-permute-start.27
  30.0 5.5 collective-permute-start.2
  34.1 4.4 collective-permute-start.3
  44.0 2.6 collective-permute-start.4
  45.3 4.3 collective-permute-start.5
  71.4 0.9 copy-start
  76.0 0.7 copy-start.4
  79.4 15.9 %collective-permute-start.6 = (f32[1,768]{1,0:T(1,128)S(1)}, f32[1,768]{1,0:T(1,128)S(1)}, u32[]{:S(2)}, u32[]{:S(2)}) collective-permute-start(f32[1,768]{1,0:T(1,128)S(1)} %get-tuple-element.937), channel_id=1, source_target_pairs={{0,32},{32,64},{64,96},{96,128},{128,160},{160,192},{192,224},{224... | collective-permute-start | bytes 9224 | tf_op jit(solution)/shard_map/ppermute | solution.py:19
  81.6 13.7 %collective-permute-start.7 = (f32[1,768]{1,0:T(1,128)S(1)}, f32[1,768]{1,0:T(1,128)S(1)}, u32[]{:S(2)}, u32[]{:S(2)}) collective-permute-start(f32[1,768]{1,0:T(1,128)S(1)} %get-tuple-element.938), channel_id=1, source_target_pairs={{32,0},{64,32},{96,64},{128,96},{160,128},{192,160},{224,192},{256... | collective-permute-start | bytes 9224 | tf_op jit(solution)/shard_map/ppermute | solution.py:22
  95.9 4.9 collective-permute-start.8
  99.2 4.4 collective-permute-start.9
  109.1 5.4 collective-permute-start.10
  113.1 6.2 collective-permute-start.11
  150.5 20.8 %collective-permute-start.12 = (f32[1,768]{1,0:T(1,128)S(1)}, f32[1,768]{1,0:T(1,128)S(1)}, u32[]{:S(2)}, u32[]{:S(2)}) collective-permute-start(f32[1,768]{1,0:T(1,128)S(1)} %get-tuple-element.929), channel_id=1, source_target_pairs={{0,32},{32,64},{64,96},{96,128},{128,160},{160,192},{192,224},{224... | collective-permute-start | bytes 9224 | tf_op jit(solution)/shard_map/ppermute | solution.py:19
  152.4 18.9 %collective-permute-start.13 = (f32[1,768]{1,0:T(1,128)S(1)}, f32[1,768]{1,0:T(1,128)S(1)}, u32[]{:S(2)}, u32[]{:S(2)}) collective-permute-start(f32[1,768]{1,0:T(1,128)S(1)} %get-tuple-element.930), channel_id=1, source_target_pairs={{32,0},{64,32},{96,64},{128,96},{160,128},{192,160},{224,192},{256... | collective-permute-start | bytes 9224 | tf_op jit(solution)/shard_map/ppermute | solution.py:22
  165.2 11.8 %collective-permute-start.28 = (f32[1,128]{1,0:T(1,128)S(1)}, f32[1,128]{1,0:T(1,128)S(1)}, u32[]{:S(2)}, u32[]{:S(2)}) collective-permute-start(f32[1,128]{1,0:T(1,128)S(1)} %get-tuple-element.995), channel_id=1, source_target_pairs={{0,1},{1,2},{2,3},{3,4},{4,5},{5,6},{6,7},{8,9},{9,10},{10,11},{11... | collective-permute-start | bytes 1544 | tf_op jit(solution)/shard_map/ppermute | solution.py:19
  170.0 7.0 collective-permute-start.29
  171.9 5.1 collective-permute-start.14
  175.2 4.4 collective-permute-start.15
  185.1 5.6 collective-permute-start.16
  189.4 4.3 collective-permute-start.17
  216.0 0.7 copy-start.3
  217.2 14.7 %collective-permute-start.18 = (f32[1,256]{1,0:T(1,128)S(1)}, f32[1,256]{1,0:T(1,128)S(1)}, u32[]{:S(2)}, u32[]{:S(2)}) collective-permute-start(f32[1,256]{1,0:T(1,128)S(1)} %get-tuple-element.991), channel_id=1, source_target_pairs={{0,32},{32,64},{64,96},{96,128},{128,160},{160,192},{192,224},{224... | collective-permute-start | bytes 3080 | tf_op jit(solution)/shard_map/ppermute | solution.py:19
  219.2 13.6 %collective-permute-start.19 = (f32[1,256]{1,0:T(1,128)S(1)}, f32[1,256]{1,0:T(1,128)S(1)}, u32[]{:S(2)}, u32[]{:S(2)}) collective-permute-start(f32[1,256]{1,0:T(1,128)S(1)} %get-tuple-element.992), channel_id=1, source_target_pairs={{32,0},{64,32},{96,64},{128,96},{160,128},{192,160},{224,192},{256... | collective-permute-start | bytes 3080 | tf_op jit(solution)/shard_map/ppermute | solution.py:22
  233.2 3.1 collective-permute-start.20
  234.9 4.3 collective-permute-start.21
  240.3 11.0 collective-permute-start.22
  243.9 7.4 collective-permute-start.23
  261.1 13.8 %collective-permute-start.30 = (f32[1,256]{1,0:T(1,128)S(1)}, f32[1,256]{1,0:T(1,128)S(1)}, u32[]{:S(2)}, u32[]{:S(2)}) collective-permute-start(f32[1,256]{1,0:T(1,128)S(1)} %get-tuple-element.985), channel_id=1, source_target_pairs={{0,32},{32,64},{64,96},{96,128},{128,160},{160,192},{192,224},{224... | collective-permute-start | bytes 3080 | tf_op jit(solution)/shard_map/ppermute | solution.py:19
  263.0 12.7 %collective-permute-start.31 = (f32[1,256]{1,0:T(1,128)S(1)}, f32[1,256]{1,0:T(1,128)S(1)}, u32[]{:S(2)}, u32[]{:S(2)}) collective-permute-start(f32[1,256]{1,0:T(1,128)S(1)} %get-tuple-element.986), channel_id=1, source_target_pairs={{32,0},{64,32},{96,64},{128,96},{160,128},{192,160},{224,192},{256... | collective-permute-start | bytes 3080 | tf_op jit(solution)/shard_map/ppermute | solution.py:22
  276.1 3.0 collective-permute-start.32
  277.8 4.3 collective-permute-start.33
  283.2 5.6 collective-permute-start.34
  287.5 4.7 collective-permute-start.35
  507.7 6.2 collective-permute-start.36
  511.9 5.2 collective-permute-start.37
  517.5 5.3 collective-permute-start.38
  521.5 4.3 collective-permute-start.39
  527.1 3.2 collective-permute-start.40
  529.0 5.0 collective-permute-start.41
  747.1 6.2 collective-permute-start.42
  751.4 5.2 collective-permute-start.43
  757.0 4.1 collective-permute-start.44
  759.8 4.3 collective-permute-start.45
  765.2 3.5 collective-permute-start.46
  767.4 5.2 collective-permute-start.47
  778.8 105.9 %copy-start.2 = (f32[1,2,1,4,8,8,8]{6,5,4,3,1,2,0:T(8,128)S(1)}, f32[1,2,1,4,8,8,8]{6,5,4,3,1,2,0:T(8,128)}, u32[]{:S(2)}) copy-start(f32[1,2,1,4,8,8,8]{6,5,4,3,1,2,0:T(8,128)} %get-tuple-element.861) | copy-start | bytes 49156
  985.5 6.2 collective-permute-start.48
  989.7 5.2 collective-permute-start.49
  995.3 4.2 collective-permute-start.50
  998.2 4.3 collective-permute-start.51
  1003.6 3.5 collective-permute-start.52
  1005.8 5.2 collective-permute-start.53
  1124.1 1.0 copy-start.1
where the time goes:
time: 1140 us; the launch traced here: 1130 us
  blocking collectives  703 us (62%)
  starting transfers between devices  176 us (15%)
  local copies, waits for them, and re-layouts  148 us (13%)
  waiting for transfers between devices  60.7 us (5%)
  matrix products  17.8 us (2%)
  between operations  13.6 us (1%)
    psum x4, blocking collectives, norm_weighted_mass(): return lax.psum(local_inner(residual_vec, precond_vec), ('gx', 'gy', 'gz'))  391 us
    psum x3, blocking collectives, body(): lax.psum(local_inner(search, applied), ('gx', 'gy', 'gz'))  312 us
    scatter x54, local copies, waits for them, and re-layouts, place_face(): return values.at[selector].set(update)  98.6 us
    ppermute x27, starting transfers between devices, extended(): lax.ppermute(lax.slice_in_dim(block, 0, width, axis=dim), axis, backward)  95.5 us
    ppermute x27, starting transfers between devices, extended(): lax.ppermute(lax.slice_in_dim(block, block.shape[dim] - width, None, axis...  80.1 us
    ppermute x27, waiting for transfers between devices, extended(): lax.ppermute(lax.slice_in_dim(block, 0, width, axis=dim), axis, backward)  60.7 us
  transfers between devices with their start and end apart: 54, of which 21 were waited for; matrix products, arithmetic and copies ran while one was open for 1% of the time, Pallas kernels for 0%

commit v1 on v0

--- a/solution.py
+++ b/solution.py
@@ -162,7 +162,13 @@
         return jnp.sum(first * second / multiplicity)
 
     def norm_weighted_mass(residual_vec, precond_vec):
-        return lax.psum(local_inner(residual_vec, precond_vec), ("gx", "gy", "gz"))
+
+        def serve_flows_here(buf, dev_axis, mesh_dim):
+            for nth in (dev_axis, mesh_dim):
+                buf = jax.lax.psum(buf, nth)
+            return buf
+
+        return serve_flows_here(local_inner(residual_vec, precond_vec), "gx", ("gy", "gz"))
 
     pressure = jnp.zeros_like(source)
     residual = source

time: 1140 us -> 1330 us (1.17)
  blocking collectives: 703 us -> 864 us
  starting transfers between devices: 176 us -> 215 us
    psum x3 -> x4, blocking collectives: 312 us -> 428 us  [body(): lax.psum(local_inner(search, applied), ('gx', 'gy', 'gz'))]
    psum x4 -> x8, blocking collectives: 391 us -> 436 us  [serve_flows_here(): buf = jax.lax.psum(buf, nth)]
    ppermute x27, starting transfers between devices: 95.5 us -> 115 us  [extended(): lax.ppermute(lax.slice_in_dim(block, 0, width, axis=dim), axis, backward)]
    ppermute x27, starting transfers between devices: 80.1 us -> 99.9 us  [extended(): lax.ppermute(lax.slice_in_dim(block, block.shape[dim] - width, None, axis...]
where the time goes in v1:
time: 1330 us; the launch traced here: 1320 us
  blocking collectives  864 us (65%)
  starting transfers between devices  215 us (16%)
  local copies, waits for them, and re-layouts  148 us (11%)
  waiting for transfers between devices  50.8 us (4%)
  matrix products  17.9 us (1%)
  between operations  13.6 us (1%)
    psum x8, blocking collectives, serve_flows_here(): buf = jax.lax.psum(buf, nth)  436 us
    psum x4, blocking collectives, body(): lax.psum(local_inner(search, applied), ('gx', 'gy', 'gz'))  428 us
    ppermute x27, starting transfers between devices, extended(): lax.ppermute(lax.slice_in_dim(block, 0, width, axis=dim), axis, backward)  115 us
    ppermute x27, starting transfers between devices, extended(): lax.ppermute(lax.slice_in_dim(block, block.shape[dim] - width, None, axis...  99.9 us
    scatter x54, local copies, waits for them, and re-layouts, place_face(): return values.at[selector].set(update)  98.7 us
    ppermute x27, waiting for transfers between devices, extended(): lax.ppermute(lax.slice_in_dim(block, 0, width, axis=dim), axis, backward)  50.7 us
  transfers between devices with their start and end apart: 54, of which 21 were waited for; matrix products, arithmetic and copies ran while one was open for 1% of the time, Pallas kernels for 0%

profile of v1, /device:TPU:1, one launch (start us, length us, event | category | flops | bytes accessed | tf_op | source)
XLA Modules:
  0.0 1318.2 jit_solution(3516431587018881805)
XLA Ops:
  2.1 4.5 collective-permute-start
  6.6 6.2 collective-permute-start.1
  15.8 9.7 collective-permute-start.25
  30.0 4.0 collective-permute-start.2
  35.4 3.0 collective-permute-done.3
  46.6 3.0 collective-permute-done.5
  51.0 2.6 scatter.186
  54.8 15.4 %scatter.189 = f32[3,2,1,4,8,8,8]{6,5,4,3,1,0,2:T(8,128)S(1)} dynamic-update-slice(f32[3,2,1,4,8,8,8]{6,5,4,3,1,0,2:T(8,128)S(1)} %scatter.186, f32[3,2,1,4,8,8,1]{6,5,4,3,1,0,2:T(8,128)S(1)} %copy.186, s32[]{:T(128)} %constant.1319.clone.1, s32[]{:T(128)} %constant.1319.clone.1, s32[]{:T(128)} %constant.1319.clone.1, s32[]{:T(128)} %constant.1319.clone.1, s32[]{:T(128)} %constant.1319.clone.1, ...) | dynamic-update-slice | bytes 12292 | tf_op jit(solution)/shard_map/scatter | solution.py:63
  76.8 2.4 fusion.2
  79.4 2.2 collective-permute-start.6
  81.7 12.9 collective-permute-start.7
  95.9 3.2 collective-permute-start.8
  100.9 2.8 collective-permute-done.9
  109.2 4.0 collective-permute-start.10
  114.6 4.7 collective-permute-done.11
  120.1 2.1 copy.201
  122.2 2.6 scatter.196
  127.6 15.4 %scatter.199 = f32[3,2,1,4,8,8,8]{6,5,4,3,1,0,2:T(8,128)S(1)} dynamic-update-slice(f32[3,2,1,4,8,8,8]{6,5,4,3,1,0,2:T(8,128)S(1)} %scatter.196, f32[3,2,1,4,8,8,1]{6,5,4,3,1,0,2:T(8,128)S(1)} %copy.203, s32[]{:T(128)} %constant.1319.clone.1, s32[]{:T(128)} %constant.1319.clone.1, s32[]{:T(128)} %constant.1319.clone.1, s32[]{:T(128)} %constant.1319.clone.1, s32[]{:T(128)} %constant.1319.clone.1, ...) | dynamic-update-slice | bytes 12292 | tf_op jit(solution)/shard_map/scatter | solution.py:63
  148.1 2.2 fusion.5
  152.5 12.7 collective-permute-start.13
  165.2 4.8 collective-permute-start.28
  172.0 3.2 collective-permute-start.14
  177.0 2.6 collective-permute-done.15
  185.2 4.3 collective-permute-start.16
  190.8 3.0 collective-permute-done.17
  195.1 2.6 scatter.206
  199.0 15.4 %scatter.209 = f32[3,2,1,4,8,8,8]{6,5,4,3,1,0,2:T(8,128)S(1)} dynamic-update-slice(f32[3,2,1,4,8,8,8]{6,5,4,3,1,0,2:T(8,128)S(1)} %scatter.206, f32[3,2,1,4,8,8,1]{6,5,4,3,1,0,2:T(8,128)S(1)} %copy.220, s32[]{:T(128)} %constant.1319.clone.1, s32[]{:T(128)} %constant.1319.clone.1, s32[]{:T(128)} %constant.1319.clone.1, s32[]{:T(128)} %constant.1319.clone.1, s32[]{:T(128)} %constant.1319.clone.1, ...) | dynamic-update-slice | bytes 12292 | tf_op jit(solution)/shard_map/scatter | solution.py:63
  219.2 12.8 collective-permute-start.19
  236.2 3.0 collective-permute-done.21
  240.3 3.6 collective-permute-start.22
  246.7 4.6 scatter.229
  252.8 4.8 scatter.219
  263.0 11.8 collective-permute-start.31
  279.2 3.0 collective-permute-done.33
  283.2 4.3 collective-permute-start.34
  288.8 3.4 collective-permute-done.35
  293.7 4.6 scatter.239
  299.1 53.5 %psum.84 = f32[]{:T(128)} all-reduce(f32[]{:T(128)} %get-tuple-element.811), channel_id=1, replica_groups=mesh['gx'=16,'gy'=4,'gz'=8] {'gx'}, use_global_device_ids=true, to_apply=%region_2.15 | all-reduce | flops 1 | bytes 8 | tf_op jit(solution)/shard_map/psum | solution.py:168
  352.7 62.8 %psum.85 = f32[]{:T(128)} all-reduce(f32[]{:T(128)} %psum.84), channel_id=1, replica_groups=mesh['gx'=16,'gy'=4,'gz'=8] {'gy','gz'}, use_global_device_ids=true, to_apply=%region_3.16 | all-reduce | flops 1 | bytes 8 | tf_op jit(solution)/shard_map/psum | solution.py:168
  415.5 111.4 %psum.86 = f32[]{:T(128)} all-reduce(f32[]{:T(128)} %get-tuple-element.810), channel_id=1, replica_groups=mesh['gx'=16,'gy'=4,'gz'=8] {'gx','gy','gz'}, use_global_device_ids=true, to_apply=%region_5.18 | all-reduce | flops 1 | bytes 8 | tf_op jit(solution)/shard_map/psum | solution.py:188
  529.0 43.4 %psum.87 = f32[]{:T(128)} all-reduce(f32[]{:T(128)} %get-tuple-element.860), channel_id=1, replica_groups=mesh['gx'=16,'gy'=4,'gz'=8] {'gx'}, use_global_device_ids=true, to_apply=%region_7.20 | all-reduce | flops 1 | bytes 8 | tf_op jit(solution)/shard_map/psum | solution.py:168
  572.4 63.5 %psum.88 = f32[]{:T(128)} all-reduce(f32[]{:T(128)} %psum.87), channel_id=1, replica_groups=mesh['gx'=16,'gy'=4,'gz'=8] {'gy','gz'}, use_global_device_ids=true, to_apply=%region_8.21 | all-reduce | flops 1 | bytes 8 | tf_op jit(solution)/shard_map/psum | solution.py:168
  640.7 13.9 %collective-permute-start.36 = (f32[1,256]{1,0:T(1,128)S(1)}, f32[1,256]{1,0:T(1,128)S(1)}, u32[]{:S(2)}, u32[]{:S(2)}) collective-permute-start(f32[1,256]{1,0:T(1,128)S(1)} %get-tuple-element.977), channel_id=1, source_target_pairs={{0,32},{32,64},{64,96},{96,128},{128,160},{160,192},{192,224},{224... | collective-permute-start | bytes 3080 | tf_op jit(solution)/shard_map/ppermute | solution.py:19
  654.6 8.6 collective-permute-start.37
  667.1 3.0 collective-permute-done.39
  674.7 3.0 collective-permute-done.41
  679.1 4.6 scatter.249
  684.5 105.7 %psum.89 = f32[]{:T(128)} all-reduce(f32[]{:T(128)} %fusion.31), channel_id=1, replica_groups=mesh['gx'=16,'gy'=4,'gz'=8] {'gx','gy','gz'}, use_global_device_ids=true, to_apply=%region_10.23 | all-reduce | flops 1 | bytes 8 | tf_op jit(solution)/shard_map/psum | solution.py:188
  793.0 43.4 %psum.90 = f32[]{:T(128)} all-reduce(f32[]{:T(128)} %get-tuple-element.857), channel_id=1, replica_groups=mesh['gx'=16,'gy'=4,'gz'=8] {'gx'}, use_global_device_ids=true, to_apply=%region_12.25 | all-reduce | flops 1 | bytes 8 | tf_op jit(solution)/shard_map/psum | solution.py:168
  836.4 62.6 %psum.91 = f32[]{:T(128)} all-reduce(f32[]{:T(128)} %psum.90), channel_id=1, replica_groups=mesh['gx'=16,'gy'=4,'gz'=8] {'gy','gz'}, use_global_device_ids=true, to_apply=%region_13.26 | all-reduce | flops 1 | bytes 8 | tf_op jit(solution)/shard_map/psum | solution.py:168
  903.8 12.4 collective-permute-start.42
  916.2 8.6 collective-permute-start.43
  928.7 3.0 collective-permute-done.45
  936.0 3.0 collective-permute-done.47
  940.4 4.6 scatter.259
  945.8 105.5 %psum.92 = f32[]{:T(128)} all-reduce(f32[]{:T(128)} %fusion.33), channel_id=1, replica_groups=mesh['gx'=16,'gy'=4,'gz'=8] {'gx','gy','gz'}, use_global_device_ids=true, to_apply=%region_15.28 | all-reduce | flops 1 | bytes 8 | tf_op jit(solution)/shard_map/psum | solution.py:188
  1054.1 43.4 %psum.93 = f32[]{:T(128)} all-reduce(f32[]{:T(128)} %get-tuple-element.854), channel_id=1, replica_groups=mesh['gx'=16,'gy'=4,'gz'=8] {'gx'}, use_global_device_ids=true, to_apply=%region_17.30 | all-reduce | flops 1 | bytes 8 | tf_op jit(solution)/shard_map/psum | solution.py:168
  1097.5 63.1 %psum.94 = f32[]{:T(128)} all-reduce(f32[]{:T(128)} %psum.93), channel_id=1, replica_groups=mesh['gx'=16,'gy'=4,'gz'=8] {'gy','gz'}, use_global_device_ids=true, to_apply=%region_18.31 | all-reduce | flops 1 | bytes 8 | tf_op jit(solution)/shard_map/psum | solution.py:168
  1165.3 12.4 collective-permute-start.48
  1177.7 8.6 collective-permute-start.49
  1190.2 3.0 collective-permute-done.51
  1197.5 3.0 collective-permute-done.53
  1201.9 4.6 scatter.269
  1208.3 105.5 %psum.95 = f32[]{:T(128)} all-reduce(f32[]{:T(128)} %fusion.35), channel_id=1, replica_groups=mesh['gx'=16,'gy'=4,'gz'=8] {'gx','gy','gz'}, use_global_device_ids=true, to_apply=%region_20.33 | all-reduce | flops 1 | bytes 8 | tf_op jit(solution)/shard_map/psum | solution.py:188
  (536 shorter events, 136.8 us)
Async XLA Ops:
  1.9 10.9 copy-start.5
  2.1 27.2 %collective-permute-start = (f32[1,768]{1,0:T(1,128)S(1)}, f32[1,768]{1,0:T(1,128)S(1)}, u32[]{:S(2)}, u32[]{:S(2)}) collective-permute-start(f32[1,768]{1,0:T(1,128)S(1)} %get-tuple-element.943), channel_id=1, source_target_pairs={{0,32},{32,64},{64,96},{96,128},{128,160},{160,192},{192,224},{224... | collective-permute-start | bytes 9224 | tf_op jit(solution)/shard_map/ppermute | solution.py:19
  6.6 22.7 %collective-permute-start.1 = (f32[1,768]{1,0:T(1,128)S(1)}, f32[1,768]{1,0:T(1,128)S(1)}, u32[]{:S(2)}, u32[]{:S(2)}) collective-permute-start(f32[1,768]{1,0:T(1,128)S(1)} %get-tuple-element.944), channel_id=1, source_target_pairs={{32,0},{64,32},{96,64},{128,96},{160,128},{192,160},{224,192},{256... | collective-permute-start | bytes 9224 | tf_op jit(solution)/shard_map/ppermute | solution.py:22
  12.8 0.7 copy-start.6
  12.9 0.7 copy-start.7
  13.9 12.1 collective-permute-start.24
  15.8 10.5 collective-permute-start.25
  26.7 8.7 collective-permute-start.26
  28.1 7.3 collective-permute-start.27
  30.0 5.5 collective-permute-start.2
  34.1 4.4 collective-permute-start.3
  44.0 2.6 collective-permute-start.4
  45.3 4.3 collective-permute-start.5
  71.4 0.9 copy-start
  76.1 0.7 copy-start.4
  79.4 15.9 %collective-permute-start.6 = (f32[1,768]{1,0:T(1,128)S(1)}, f32[1,768]{1,0:T(1,128)S(1)}, u32[]{:S(2)}, u32[]{:S(2)}) collective-permute-start(f32[1,768]{1,0:T(1,128)S(1)} %get-tuple-element.935), channel_id=1, source_target_pairs={{0,32},{32,64},{64,96},{96,128},{128,160},{160,192},{192,224},{224... | collective-permute-start | bytes 9224 | tf_op jit(solution)/shard_map/ppermute | solution.py:19
  81.7 13.7 %collective-permute-start.7 = (f32[1,768]{1,0:T(1,128)S(1)}, f32[1,768]{1,0:T(1,128)S(1)}, u32[]{:S(2)}, u32[]{:S(2)}) collective-permute-start(f32[1,768]{1,0:T(1,128)S(1)} %get-tuple-element.936), channel_id=1, source_target_pairs={{32,0},{64,32},{96,64},{128,96},{160,128},{192,160},{224,192},{256... | collective-permute-start | bytes 9224 | tf_op jit(solution)/shard_map/ppermute | solution.py:22
  95.9 4.9 collective-permute-start.8
  99.3 4.4 collective-permute-start.9
  109.2 5.4 collective-permute-start.10
  113.2 6.2 collective-permute-start.11
  150.5 20.8 %collective-permute-start.12 = (f32[1,768]{1,0:T(1,128)S(1)}, f32[1,768]{1,0:T(1,128)S(1)}, u32[]{:S(2)}, u32[]{:S(2)}) collective-permute-start(f32[1,768]{1,0:T(1,128)S(1)} %get-tuple-element.927), channel_id=1, source_target_pairs={{0,32},{32,64},{64,96},{96,128},{128,160},{160,192},{192,224},{224... | collective-permute-start | bytes 9224 | tf_op jit(solution)/shard_map/ppermute | solution.py:19
  152.5 18.9 %collective-permute-start.13 = (f32[1,768]{1,0:T(1,128)S(1)}, f32[1,768]{1,0:T(1,128)S(1)}, u32[]{:S(2)}, u32[]{:S(2)}) collective-permute-start(f32[1,768]{1,0:T(1,128)S(1)} %get-tuple-element.928), channel_id=1, source_target_pairs={{32,0},{64,32},{96,64},{128,96},{160,128},{192,160},{224,192},{256... | collective-permute-start | bytes 9224 | tf_op jit(solution)/shard_map/ppermute | solution.py:22
  165.2 11.8 collective-permute-start.28
  170.1 6.9 collective-permute-start.29
  172.0 5.1 collective-permute-start.14
  175.3 4.4 collective-permute-start.15
  185.2 5.6 collective-permute-start.16
  189.4 4.3 collective-permute-start.17
  216.0 0.7 copy-start.3
  217.2 14.7 %collective-permute-start.18 = (f32[1,256]{1,0:T(1,128)S(1)}, f32[1,256]{1,0:T(1,128)S(1)}, u32[]{:S(2)}, u32[]{:S(2)}) collective-permute-start(f32[1,256]{1,0:T(1,128)S(1)} %get-tuple-element.989), channel_id=1, source_target_pairs={{0,32},{32,64},{64,96},{96,128},{128,160},{160,192},{192,224},{224... | collective-permute-start | bytes 3080 | tf_op jit(solution)/shard_map/ppermute | solution.py:19
  219.2 13.6 %collective-permute-start.19 = (f32[1,256]{1,0:T(1,128)S(1)}, f32[1,256]{1,0:T(1,128)S(1)}, u32[]{:S(2)}, u32[]{:S(2)}) collective-permute-start(f32[1,256]{1,0:T(1,128)S(1)} %get-tuple-element.990), channel_id=1, source_target_pairs={{32,0},{64,32},{96,64},{128,96},{160,128},{192,160},{224,192},{256... | collective-permute-start | bytes 3080 | tf_op jit(solution)/shard_map/ppermute | solution.py:22
  233.2 3.0 collective-permute-start.20
  234.9 4.3 collective-permute-start.21
  240.3 11.0 collective-permute-start.22
  243.9 7.4 collective-permute-start.23
  261.1 13.8 %collective-permute-start.30 = (f32[1,256]{1,0:T(1,128)S(1)}, f32[1,256]{1,0:T(1,128)S(1)}, u32[]{:S(2)}, u32[]{:S(2)}) collective-permute-start(f32[1,256]{1,0:T(1,128)S(1)} %get-tuple-element.983), channel_id=1, source_target_pairs={{0,32},{32,64},{64,96},{96,128},{128,160},{160,192},{192,224},{224... | collective-permute-start | bytes 3080 | tf_op jit(solution)/shard_map/ppermute | solution.py:19
  263.0 12.7 collective-permute-start.31
  276.1 3.0 collective-permute-start.32
  277.8 4.3 collective-permute-start.33
  283.2 5.6 collective-permute-start.34
  287.5 4.7 collective-permute-start.35
  640.7 22.4 %collective-permute-start.36 = (f32[1,256]{1,0:T(1,128)S(1)}, f32[1,256]{1,0:T(1,128)S(1)}, u32[]{:S(2)}, u32[]{:S(2)}) collective-permute-start(f32[1,256]{1,0:T(1,128)S(1)} %get-tuple-element.977), channel_id=1, source_target_pairs={{0,32},{32,64},{64,96},{96,128},{128,160},{160,192},{192,224},{224... | collective-permute-start | bytes 3080 | tf_op jit(solution)/shard_map/ppermute | solution.py:19
  654.6 9.4 collective-permute-start.37
  664.4 2.7 collective-permute-start.38
  665.7 4.3 collective-permute-start.39
  671.4 3.3 collective-permute-start.40
  673.4 4.3 collective-permute-start.41
  903.8 21.0 %collective-permute-start.42 = (f32[1,256]{1,0:T(1,128)S(1)}, f32[1,256]{1,0:T(1,128)S(1)}, u32[]{:S(2)}, u32[]{:S(2)}) collective-permute-start(f32[1,256]{1,0:T(1,128)S(1)} %get-tuple-element.971), channel_id=1, source_target_pairs={{0,32},{32,64},{64,96},{96,128},{128,160},{160,192},{192,224},{224... | collective-permute-start | bytes 3080 | tf_op jit(solution)/shard_map/ppermute | solution.py:19
  916.2 9.4 collective-permute-start.43
  926.0 2.7 collective-permute-start.44
  927.4 4.3 collective-permute-start.45
  932.8 3.1 collective-permute-start.46
  934.6 4.3 collective-permute-start.47
  945.1 107.6 %copy-start.2 = (f32[1,2,1,4,8,8,8]{6,5,4,3,1,2,0:T(8,128)S(1)}, f32[1,2,1,4,8,8,8]{6,5,4,3,1,2,0:T(8,128)}, u32[]{:S(2)}) copy-start(f32[1,2,1,4,8,8,8]{6,5,4,3,1,2,0:T(8,128)} %get-tuple-element.859) | copy-start | bytes 49156
  1165.3 21.0 %collective-permute-start.48 = (f32[1,256]{1,0:T(1,128)S(1)}, f32[1,256]{1,0:T(1,128)S(1)}, u32[]{:S(2)}, u32[]{:S(2)}) collective-permute-start(f32[1,256]{1,0:T(1,128)S(1)} %get-tuple-element.965), channel_id=1, source_target_pairs={{0,32},{32,64},{64,96},{96,128},{128,160},{160,192},{192,224},{224... | collective-permute-start | bytes 3080 | tf_op jit(solution)/shard_map/ppermute | solution.py:19
  1177.7 9.4 collective-permute-start.49
  1187.5 2.7 collective-permute-start.50
  1188.9 4.3 collective-permute-start.51
  1194.3 3.1 collective-permute-start.52
  1196.2 4.3 collective-permute-start.53
  1315.2 1.0 copy-start.1
